TPU v7x, 128 devices: a whole 4x4x4 slice. The times are simulated.
128 devices in a mesh: req: 16 (over y, x), seq: 4 (over z), hid: 2 (over core).
Axes of the slice: x: 4, y: 4, z: 4, core: 2. Of those that a mesh axis runs over, the one named last changes fastest.
Arguments:
- tokens: bfloat16 [65536, 2048], P(('req', 'seq')), may hold values from -6 to 6
- attention_gain: bfloat16 [2048], replicated, may hold values from 0.099609375 to 1.8984375
- project_weight: bfloat16 [2048, 2048], P(None, 'hid'), may hold values from -0.125 to 0.125
- conv_weight: bfloat16 [4, 2048], P(None, 'hid'), may hold values from -3 to 3
- decay_down: bfloat16 [2048, 16], replicated, may hold values from -0.125 to 0.125
- decay_up: bfloat16 [16, 512], P(None, 'hid'), may hold values from -1.5 to 1.5
- decay_bias: float32 [512], P('hid'), may hold values from -2 to 10
- output_gate: bfloat16 [2048, 1024], P(None, 'hid'), may hold values from -0.125 to 0.125
- head_gain: bfloat16 [512], replicated, may hold values from 0.099609375 to 1.8984375
- output_weight: bfloat16 [1024, 2048], P('hid'), may hold values from -0.1875 to 0.1875
- mixer_gain: bfloat16 [2048], replicated, may hold values from 0.099609375 to 1.8984375
- gate_weight: bfloat16 [2048, 2816], P('req', 'hid'), may hold values from -0.125 to 0.125
- up_weight: bfloat16 [2048, 2816], P('req', 'hid'), may hold values from -0.125 to 0.125
- down_weight: bfloat16 [2816, 2048], P('hid', 'req'), may hold values from -0.109375 to 0.109375
- prompt_pages: int32 [16, 16], P('req'), may hold values from 0 to 64, as said below
- prompt_start: int32 [16, 16], P('req'), may hold values from 0 to 63, as said below
Outputs:
- hidden_out: bfloat16 [65536, 2048], P(('req', 'seq', 'hid'))
- page_states: bfloat16 [1024, 2, 256, 512], P(('req', 'seq'), 'hid')
- conv_edges: bfloat16 [1024, 3, 2048], P(('req', 'seq'), None, 'hid')
Inputs may be any that keep to these rules, and one draw needn't show every extreme that they name: `prompt_pages`: row r lists the page counts of the prompts of group r; 0 marks an unused slot; in every draw some group holds one prompt of all its 64 pages. `prompt_start`: the slots of a row that are used cover pages in increasing order without intersection and end by page 64; pages between prompts belong to none; an unused slot starts at page 64 - 1, and every draw has one.
All inputs are finite; a program needn't handle non-finite values.
Results may differ from a plain program's by a relative error of at most 0.014.
Values may be sent and summed in bfloat16 or wider, within the bound.
A program may use at most 192 MiB of HBM per device.

v0:
```python
import jax
import jax.numpy as jnp
from jax import lax
from jax.sharding import PartitionSpec as P

HK = 256
HV = 512
KCONV = 4
PAGE = 64
CONVW = 1024
EPSILON = 1e-06
TOP_PRECISION = lax.Precision.HIGHEST


def shifted(value, axis, steps):
    count = lax.axis_size(axis)
    first, last = (max(0, -steps), min(count, count - steps))
    return lax.ppermute(value, axis, [(source, source + steps) for source in range(first, last)])


def prefix_2(array, axis, join, neutral):
    place = lax.axis_index(axis)
    gathered = jax.tree.map(
        lambda a, kind: lax.all_gather(a.astype(kind), axis), array, (jnp.bfloat16, jnp.bfloat16)
    )
    state = jax.tree.map(lambda a, e: jnp.zeros_like(a) + jnp.asarray(e, a.dtype), array, neutral)

    def one(lap, state):
        return join(
            state,
            jax.tree.map(
                lambda a, own: lax.dynamic_index_in_dim(a, lap, 0, False).astype(own.dtype),
                gathered,
                array,
            ),
        )

    return lax.fori_loop(0, place, one, state)


def rms_scaled(values, scale_gain):
    values = values.astype(jnp.float32)
    return (
        values
        * lax.rsqrt(jnp.mean(values * values, axis=-1, keepdims=True) + EPSILON)
        * scale_gain.astype(jnp.float32)
    )


def page_segments(page_counts, starts, total_pages):
    position = jnp.arange(total_pages, dtype=jnp.int32)
    inside = (position[None, :] >= starts[:, None]) & (
        position[None, :] < starts[:, None] + page_counts[:, None]
    )
    labels = jnp.arange(1, page_counts.shape[0] + 1, dtype=jnp.int32)
    segment = jnp.sum(jnp.where(inside, labels[:, None], 0), axis=0) - 1
    earlier = jnp.concatenate([jnp.full((1,), -1, jnp.int32), segment[:-1]])
    return ((segment == earlier) & (segment >= 0)).astype(jnp.float32)


def short_conv(by_page, before, carried, conv_taps):
    kept_rows = before.astype(jnp.float32) * carried[:, None, None]
    widened = jnp.concatenate([kept_rows, by_page.astype(jnp.float32)], axis=1)
    tap_count = conv_taps.shape[0]
    length = by_page.shape[1]
    result = jnp.zeros(by_page.shape, jnp.float32)
    for offset in range(tap_count):
        result = (
            result
            + conv_taps[offset].astype(jnp.float32)
            * widened[:, tap_count - 1 - offset : tap_count - 1 - offset + length]
        )
    return result


def split_features(mixed_rows, key_width):
    query_rows = jax.nn.silu(mixed_rows[..., :key_width])
    key_rows = jax.nn.silu(mixed_rows[..., key_width : 2 * key_width]) * key_width ** (-0.5)
    value_matrix = mixed_rows[..., 2 * key_width :]
    return (
        query_rows.transpose(0, 2, 1, 3),
        key_rows.transpose(0, 2, 1, 3),
        value_matrix.transpose(0, 2, 1, 3),
    )


def page_block(query_rows, key_rows, value_matrix, decay_sum, carried):
    length = query_rows.shape[2]
    page_count = query_rows.shape[0]
    raised_rows = query_rows * jnp.exp(decay_sum)
    lowered = key_rows * jnp.exp(-decay_sum)
    scores = jnp.einsum("phik,phjk->phij", raised_rows, lowered, precision=TOP_PRECISION)
    rows_index = jnp.arange(length)
    causal = rows_index[:, None] >= rows_index[None, :]
    scores = jnp.where(causal[None, None], scores, 0.0)
    layer_output = jnp.einsum("phij,phjv->phiv", scores, value_matrix, precision=TOP_PRECISION)
    closing_sum = decay_sum[:, :, -1, :]
    weighted_rows = key_rows * jnp.exp(closing_sum[:, :, None, :] - decay_sum)
    page_terms = jnp.einsum("phte,phtb->pheb", weighted_rows, value_matrix, precision=TOP_PRECISION)
    through = jnp.cumsum(closing_sum, axis=0)
    resets = jnp.cumsum(1.0 - carried)
    pages = jnp.arange(page_count)
    valid = (pages[:, None] >= pages[None, :]) & (resets[:, None] == resets[None, :])
    spread = through[:, None] - through[None, :]
    spread = jnp.where(valid[:, :, None, None], spread, 0.0)
    weights = jnp.where(valid[:, :, None, None], jnp.exp(spread), 0.0)
    memories = jnp.einsum("pqhe,qheb->pheb", weights, page_terms, precision=TOP_PRECISION)
    previous = jnp.concatenate([jnp.zeros_like(memories[:1]), memories[:-1]], axis=0)
    previous = previous * carried[:, None, None, None]
    layer_output = layer_output + jnp.einsum(
        "phik,phkv->phiv", raised_rows, previous, precision=TOP_PRECISION
    )
    return (memories[-1], layer_output, memories)


def on_device(
    tokens,
    attention_gain,
    project_weight,
    conv_weight,
    decay_down,
    decay_up,
    decay_bias,
    output_gate,
    head_gain,
    output_weight,
    mixer_gain,
    gate_weight,
    up_weight,
    down_weight,
    prompt_pages,
    prompt_start,
):
    token_count = tokens.shape[0]
    page_count = token_count // PAGE
    local_heads = project_weight.shape[1] // CONVW
    rim_rows = KCONV - 1
    seq_index = lax.axis_index("seq")
    group_pages = page_count * lax.axis_size("seq")
    page_flags = page_segments(prompt_pages[0], prompt_start[0], group_pages)
    carried = lax.dynamic_slice_in_dim(page_flags, seq_index * page_count, page_count)
    normed = rms_scaled(tokens, attention_gain).astype(jnp.bfloat16)
    projected = jnp.dot(normed, project_weight, preferred_element_type=jnp.float32).astype(
        jnp.bfloat16
    )
    by_page = projected.reshape(page_count, PAGE, local_heads * CONVW)
    incoming = shifted(by_page[-1, PAGE - rim_rows :], "seq", 1)
    before = jnp.concatenate([incoming[None], by_page[:-1, PAGE - rim_rows :]], axis=0)
    mixed_rows = short_conv(by_page, before, carried, conv_weight).reshape(
        page_count, PAGE, local_heads, CONVW
    )
    query_rows, key_rows, value_matrix = split_features(mixed_rows, HK)
    gate_rows = lax.all_gather(gate_weight, "req", axis=0, tiled=True)
    up_rows = lax.all_gather(up_weight, "req", axis=0, tiled=True)
    down_columns = lax.all_gather(down_weight, "req", axis=1, tiled=True)
    gate_rows, query_rows = lax.optimization_barrier((gate_rows, query_rows))
    lowrank = jnp.dot(normed, decay_down, preferred_element_type=jnp.float32).astype(jnp.bfloat16)
    decay_log = (
        jax.nn.log_sigmoid(
            jnp.dot(lowrank, decay_up, preferred_element_type=jnp.float32) + decay_bias
        )
        / 16.0
    )
    decay_log = decay_log.reshape(page_count, PAGE, local_heads, HK).transpose(0, 2, 1, 3)
    decay_sum = jnp.cumsum(decay_log, axis=2)
    local_memory, outputs, memories = page_block(
        query_rows, key_rows, value_matrix, decay_sum, carried
    )
    totals = decay_sum[:, :, -1, :]
    through = jnp.cumsum(totals, axis=0)
    alive_mask = jnp.cumprod(carried)
    block_decay = alive_mask[-1] * jnp.exp(through[-1])

    def compose(earlier, latter):
        return (earlier[0] * latter[0], latter[0][..., None] * earlier[1] + latter[1])

    prefix = prefix_2(
        (block_decay, local_memory),
        "seq",
        compose,
        (jnp.ones_like(block_decay), jnp.zeros_like(local_memory)),
    )
    incoming_state = prefix[1]
    before_sum = through - totals
    extent_factor = alive_mask[:, None, None, None] * jnp.exp(decay_sum + before_sum[:, :, None, :])
    outputs = outputs + jnp.einsum(
        "dlof,lfg->dlog", query_rows * extent_factor, incoming_state, precision=TOP_PRECISION
    )
    memories = (
        memories + (alive_mask[:, None, None] * jnp.exp(through))[..., None] * incoming_state[None]
    )
    up_rows, outputs = lax.optimization_barrier((up_rows, outputs))
    attended = outputs.transpose(0, 2, 1, 3).reshape(token_count, local_heads, HV)
    normed_heads = rms_scaled(attended, head_gain)
    opening = jax.nn.silu(jnp.dot(normed, output_gate, preferred_element_type=jnp.float32)).reshape(
        token_count, local_heads, HV
    )
    gated_rows = (
        (normed_heads * opening).astype(jnp.bfloat16).reshape(token_count, local_heads * HV)
    )
    down_columns, gated_rows = lax.optimization_barrier((down_columns, gated_rows))
    partial_value = jnp.dot(gated_rows, output_weight, preferred_element_type=jnp.float32)
    half_rows = token_count // lax.axis_size("hid")
    row_start = lax.axis_index("hid") * half_rows
    mixed_sum = lax.psum(partial_value.astype(jnp.bfloat16), "hid").astype(jnp.float32)
    residual = (tokens.astype(jnp.float32) + mixed_sum).astype(jnp.bfloat16)
    feed_in = rms_scaled(residual, mixer_gain).astype(jnp.bfloat16)
    own_residual = lax.dynamic_slice_in_dim(residual, row_start, half_rows, 0)

    def widen(weight_rows):
        return jnp.dot(feed_in, weight_rows, preferred_element_type=jnp.float32)

    gate_part = widen(gate_rows)
    up_part = widen(up_rows)
    hidden = (jax.nn.silu(gate_part) * up_part).astype(jnp.bfloat16)
    partials = jnp.dot(hidden, down_columns, preferred_element_type=jnp.float32)
    feed_sum = lax.psum_scatter(
        partials.astype(jnp.bfloat16), "hid", scatter_dimension=0, tiled=True
    ).astype(jnp.float32)
    result = (own_residual.astype(jnp.float32) + feed_sum).astype(jnp.bfloat16)
    return (result, memories.astype(jnp.bfloat16), by_page[:, PAGE - rim_rows :])


def solution(mesh):
    return jax.shard_map(
        on_device,
        mesh=mesh,
        in_specs=(
            P(("req", "seq"), None),
            P(),
            P(None, "hid"),
            P(None, "hid"),
            P(),
            P(None, "hid"),
            P("hid"),
            P(None, "hid"),
            P(),
            P("hid", None),
            P(),
            P("req", "hid"),
            P("req", "hid"),
            P("hid", "req"),
            P("req", None),
            P("req", None),
        ),
        out_specs=(
            P(("req", "seq", "hid"), None),
            P(("req", "seq"), "hid", None, None),
            P(("req", "seq"), None, "hid"),
        ),
        check_vma=False,
    )
```

profile of v0, /device:TPU:1, one launch (start us, length us, event | category | flops | bytes accessed | tf_op | source)
XLA Modules:
  0.0 392.0 jit_solution(12662995687886767372)
XLA Ops:
  7.2 3.2 fusion.3
  10.5 0.3 copy-done.7
  10.8 7.3 %convolution_convert_fusion.2 = bf16[1024,1024]{1,0:T(8,128)(2,1)S(1)} fusion(bf16[2048,1024]{1,0:T(8,128)(2,1)} %param.20, bf16[1024,2048]{1,0:T(8,128)(2,1)S(1)} %copy-done.7, f32[2048]{0:T(1024)S(1)} %convert_element_type.149, f32[1024]{0:T(1024)S(1)} %add_rsqrt_fusion.2), kind=kOutput, calls=%fused_computation.53 | convolution fusion | flops 4304404480 | bytes 10498048 | tf_op jit(solution)/shard_map/dot_general | solution.py:143
  18.1 1.3 copy-done.10
  19.4 4.4 %collective-permute-start = (bf16[3,1024]{1,0:T(4,128)(2,1)S(1)}, bf16[3,1024]{1,0:T(4,128)(2,1)S(1)}, u32[]{:S(2)}, u32[]{:S(2)}) collective-permute-start(bf16[3,1024]{1,0:T(4,128)(2,1)S(1)} %slice_bitcast_fusion.5), channel_id=1, source_target_pairs={{0,2},{2,4},{4,6},{1,3},{3,5},{5,7},{8,10},{10,12},{12,14},{9,11},... | collective-permute-start | bytes 18440 | tf_op jit(solution)/shard_map/ppermute | solution.py:18
  24.0 5.2 %fusion.37 = f32[1024,256]{1,0:T(8,128)} fusion(bf16[16,256]{1,0:T(8,128)(2,1)S(1)} %copy-done.18, bf16[2048,16]{0,1:T(8,128)(2,1)S(1)} %copy-done.17, f32[256]{0:T(256)S(1)} %copy-done.19, bf16[1024,2048]{1,0:T(8,128)(2,1)} %param.18, f32[2048]{0:T(1024)S(1)} %convert_element_type.149, f32[1024]{0:T(1024)S(1)} %add_rsqrt_fusion.2), kind=kOutput, calls=%fused_computation.60 | convolution fusion | flops 86523904 | bytes 5329920 | tf_op jit(solution)/shard_map/dot_general | solution.py:160
  29.2 1.8 fusion.49
  31.4 0.1 reduce.2
  31.6 1.0 slice.80
  32.6 4.1 %convert_element_type.152 = f32[16,64,1024]{2,1,0:T(8,128)} convert(bf16[16,64,1024]{2,1,0:T(8,128)(2,1)} %bitcast.123) | non-fusion elementwise | flops 1048576 | bytes 6291456 | tf_op jit(solution)/shard_map/convert_element_type | solution.py:63
  36.9 7.6 %fusion.15 = f32[16,64,1,1024]{3,1,0,2:T(8,128)S(1)} fusion(f32[16,64,1024]{2,1,0:T(8,128)} %convert_element_type.152, f32[16,3,1024]{2,1,0:T(4,128)S(1)} %convert_multiply_fusion.4, f32[1024]{0:T(1024)S(1)} %bitcast.130, f32[1024]{0:T(1024)S(1)} %bitcast.131, f32[1024]{0:T(1024)S(1)} %bitcast.129, f32[1024]{0:T(1024)S(1)} %bitcast.128), kind=kLoop, calls=%fused_computation.29 | loop fusion | flops 10485760 | bytes 8601600 | tf_op jit(solution)/shard_map/reshape | solution.py:149
  44.6 7.4 %fusion.30 = f32[16,256,512]{2,1,0:T(8,128)S(1)} fusion(f32[16,64,1,1024]{3,1,0,2:T(8,128)S(1)} %fusion.15, f32[16,1,64,256]{3,0,1,2:T(8,128)S(1)} %fusion.49, f32[16,256]{1,0:T(8,128)S(1)} %get-tuple-element.97), kind=kOutput, calls=%fused_computation.51 | convolution fusion | flops 1612447744 | bytes 12599296 | tf_op jit(solution)/shard_map/phte,phtb->pheb/dot_general | solution.py:99
  52.0 13.6 %fusion.20 = f32[16,1,256,512]{3,0,2,1:T(8,128)S(1)} fusion(f32[16,256,512]{2,1,0:T(8,128)S(1)} %fusion.30, f32[16,256]{0,1:T(8,128)S(1)} %bitcast.125, pred[16,16]{1,0:T(8,128)(4,1)S(1)} %fusion.72), kind=kOutput, calls=%fused_computation.38 | convolution fusion | flops 402849792 | bytes 16793856 | tf_op jit(solution)/shard_map/pqhe,qheb->pheb/dot_general | solution.py:107
  65.6 3.2 copy-done.2
  68.8 0.6 slice.145
  69.4 0.7 copy.72
  70.2 0.7 all-gather.9.cloned.1.call-update
  70.9 0.7 all-gather.7.cloned.1.call-update
  71.7 0.5 all-gather.5.cloned.1.call-update
  72.4 0.5 slice.90
  73.0 0.6 fusion.74
  73.7 6.9 %all_gather.20 = bf16[4,1,256]{2,1,0:T(2,128)(2,1)S(1)} all-gather(bf16[1,1,256]{2,1,0:T(2,128)(2,1)S(1)} %fusion.74), channel_id=1, replica_groups=mesh['req'=16,'seq'=4,'hid'=2] {'seq'}, dimensions={0}, use_global_device_ids=true | all-gather | bytes 2560 | tf_op jit(solution)/shard_map/all_gather | solution.py:24
  80.6 2.5 multiply_bitcast_fusion.1
  83.1 8.6 %multiply_bitcast_fusion = f32[16,256,512]{2,0,1:T(8,128)} fusion(f32[15,1,256,512]{3,0,2,1:T(8,128)} %bitcast.119, f32[16]{0:T(128)S(1)} %get-tuple-element.95), kind=kLoop, calls=%fused_computation.19 | loop fusion | flops 2097152 | bytes 16252992 | tf_op jit(solution)/shard_map/reshape.33
  91.7 4.1 %all-gather.11.cloned.1.call-done = bf16[4,1,256,512]{3,2,1,0:T(8,128)(2,1)} async-done(((bf16[1,1,256,512]{3,2,1,0:T(8,128)(2,1)}), bf16[4,1,256,512]{3,2,1,0:T(8,128)(2,1)}) %all-gather.11.cloned.1.call-update) | async-done | bytes 1048592 | tf_op jit(solution)/shard_map/all_gather | solution.py:24
  95.8 0.2 while.12
  96.0 62.0 %all-gather.9.cloned.1.call-done = bf16[2048,1408]{1,0:T(8,128)(2,1)} async-done(((bf16[128,1408]{1,0:T(8,128)(2,1)}), bf16[2048,1408]{1,0:T(8,128)(2,1)}) %all-gather.9.cloned.1.call-update) | async-done | bytes 5767184 | tf_op jit(solution)/shard_map/all_gather | solution.py:153
  158.0 4.7 %convolution_select_fusion = f32[16,64,64]{2,1,0:T(8,128)S(1)} fusion(f32[16,1,64,256]{3,2,0,1:T(8,128)} %multiply_bitcast_fusion.1, f32[16,1,64,256]{3,0,1,2:T(8,128)} %copy-done.5, pred[64,64]{1,0:T(8,128)(4,1)S(1)} %iota_compare_fusion, f32[16,64,1,1024]{3,1,0,2:T(8,128)} %copy-done.4), kind=kOutput, calls=%fused_computation.56 | convolution fusion | flops 203489280 | bytes 4460544 | tf_op jit(solution)/shard_map/phik,phjk->phij/dot_general | solution.py:92
  162.7 3.4 fusion.31
  166.2 10.6 %fusion.7 = f32[16,64,512]{2,1,0:T(8,128)S(1)} fusion(f32[16,256,512]{2,0,1:T(8,128)S(1)} %copy-done.3, f32[16,1,64,256]{3,2,0,1:T(8,128)S(1)} %copy-done.8, f32[16,1,64,256]{3,0,1,2:T(8,128)S(1)} %copy-done.6), kind=kOutput, calls=%fused_computation.14 | convolution fusion | flops 1610874880 | bytes 12582912 | tf_op jit(solution)/shard_map/phik,phkv->phiv/dot_general | solution.py:110
  176.7 3.9 bitcast_add_fusion
  180.6 38.0 %all-gather.7.cloned.1.call-done = bf16[2048,1408]{1,0:T(8,128)(2,1)} async-done(((bf16[128,1408]{1,0:T(8,128)(2,1)}), bf16[2048,1408]{1,0:T(8,128)(2,1)}) %all-gather.7.cloned.1.call-update) | async-done | bytes 5767184 | tf_op jit(solution)/shard_map/all_gather | solution.py:154
  218.6 1.8 multiply_reduce_fusion
  220.5 7.1 %fusion.25 = bf16[1024,512]{1,0:T(8,128)(2,1)} fusion(f32[16,1,64,512]{3,2,0,1:T(8,128)} %bitcast_add_fusion, f32[512]{0:T(512)S(1)} %convert_element_type.163, f32[1024]{0:T(1024)S(1)} %rsqrt.29, bf16[2048,512]{1,0:T(8,128)(2,1)} %param.25, bf16[1024,2048]{1,0:T(8,128)(2,1)} %param.18, f32[2048]{0:T(1024)S(1)} %convert_element_type.149, ...), kind=kOutput, calls=%fused_computation.45 | convolution fusion | flops 2160066560 | bytes 9455616 | tf_op jit(solution)/shard_map/dot_general | solution.py:195
  227.6 56.9 %all-gather.5.cloned.1.call-done = bf16[1408,2048]{1,0:T(8,128)(2,1)} async-done(((bf16[1408,128]{1,0:T(8,128)(2,1)}), bf16[1408,2048]{1,0:T(8,128)(2,1)}) %all-gather.5.cloned.1.call-update) | async-done | bytes 5767184 | tf_op jit(solution)/shard_map/all_gather | solution.py:155
  284.5 5.6 %convolution_convert_fusion.1 = bf16[1024,2048]{1,0:T(8,128)(2,1)} fusion(bf16[1024,512]{1,0:T(8,128)(2,1)} %fusion.25, bf16[512,2048]{1,0:T(8,128)(2,1)S(1)} %copy-done), kind=kOutput, calls=%fused_computation.37 | convolution fusion | flops 2149580800 | bytes 7340032 | tf_op jit(solution)/shard_map/dot_general | solution.py:202
  290.2 0.6 copy-done.13
  290.8 34.2 %all-reduce.3.cloned.1.call-done = bf16[1024,2048]{1,0:T(8,128)(2,1)} async-done(((bf16[1024,2048]{1,0:T(8,128)(2,1)}), bf16[1024,2048]{1,0:T(8,128)(2,1)}) %all-reduce.3.cloned.1.call-update) | async-done | bytes 4194320 | tf_op jit(solution)/shard_map/psum | solution.py:205
  325.0 5.5 %fusion = (f32[1024]{0:T(1024)S(1)}, bf16[1024,2048]{1,0:T(8,128)(2,1)S(1)}) fusion(bf16[1024,2048]{1,0:T(8,128)(2,1)} %all-reduce.3.cloned.1.call-done, bf16[1024,2048]{1,0:T(8,128)(2,1)} %param.18), kind=kLoop, calls=%fused_computation.7 | loop fusion | flops 14679040 | bytes 12587008 | tf_op jit(solution)/shard_map/reduce_sum | solution.py:45
  330.5 2.0 copy-done.9
  332.5 10.7 %fusion.34 = f32[1024,1408]{1,0:T(8,128)} fusion(bf16[2048,1408]{1,0:T(8,128)(2,1)} %all-gather.9.cloned.1.call-done, bf16[1024,2048]{1,0:T(8,128)(2,1)S(1)} %get-tuple-element.93, f32[2048]{0:T(1024)S(1)} %convert_element_type.170, f32[1024]{0:T(1024)S(1)} %add_rsqrt_fusion.1), kind=kOutput, calls=%fused_computation.57 | convolution fusion | flops 5913968640 | bytes 15740928 | tf_op jit(solution)/shard_map/dot_general | solution.py:211
  343.2 20.9 %convolution_convert_fusion = bf16[1024,2048]{1,0:T(8,128)(2,1)} fusion(bf16[1408,2048]{1,0:T(8,128)(2,1)} %all-gather.5.cloned.1.call-done, f32[1024,1408]{1,0:T(8,128)} %fusion.34, bf16[2048,1408]{1,0:T(8,128)(2,1)} %all-gather.7.cloned.1.call-done, bf16[1024,2048]{1,0:T(8,128)(2,1)} %copy-done.9, f32[2048]{0:T(1024)S(1)} %convert_element_type.170, ...), kind=kOutput, calls=%fused_computation.36 | convolution fusion | flops 11830296576 | bytes 25702400 | tf_op jit(solution)/shard_map/dot_general | solution.py:216
  364.1 1.0 slice.93
  365.3 0.7 copy.76
  366.0 4.0 %add_convert_fusion = bf16[16,1,256,512]{3,0,2,1:T(8,128)(2,1)S(1)} fusion(f32[16,1,256,512]{3,0,2,1:T(8,128)} %copy-done.2, f32[256,512]{1,0:T(8,128)S(1)} %bitcast.120, f32[16,256]{0,1:T(8,128)S(1)} %copy.74), kind=kLoop, calls=%fused_computation.18 | loop fusion | flops 6291456 | bytes 13123584 | tf_op jit(solution)/shard_map/convert_element_type | solution.py:221
  370.0 4.5 %copy.75 = bf16[16,1,256,512]{3,2,1,0:T(8,128)(2,1)} copy(bf16[16,1,256,512]{3,0,2,1:T(8,128)(2,1)S(1)} %add_convert_fusion) | data formatting | bytes 8388608
  374.5 5.8 %reduce-scatter.2.cloned.1.call-done = bf16[512,2048]{1,0:T(8,128)(2,1)} async-done(((bf16[1024,2048]{1,0:T(8,128)(2,1)}), bf16[512,2048]{1,0:T(8,128)(2,1)}) %reduce-scatter.2.cloned.1.call-update) | async-done | bytes 2097168 | tf_op jit(solution)/shard_map/reduce_scatter | solution.py:217
  380.3 4.4 %add_convert_fusion.1 = bf16[512,2048]{1,0:T(8,128)(2,1)} fusion(bf16[512,2048]{1,0:T(8,128)(2,1)} %reduce-scatter.2.cloned.1.call-done, bf16[1024,2048]{1,0:T(8,128)(2,1)} %copy-done.9, s32[]{:T(128)S(6)} %select_n.46), kind=kLoop, calls=%fused_computation.35 | loop fusion | flops 4194304 | bytes 6291460 | tf_op jit(solution)/shard_map/convert_element_type | solution.py:220
  (74 shorter events, 1.7 us)
Async XLA Ops:
  7.2 277.4 %copy-start = (bf16[512,2048]{1,0:T(8,128)(2,1)S(1)}, bf16[512,2048]{1,0:T(8,128)(2,1)}, u32[]{:S(2)}) copy-start(bf16[512,2048]{1,0:T(8,128)(2,1)} %param.27) | copy-start | bytes 6291460
  7.2 3.3 copy-start.12
  7.2 88.6 %all-gather.11.cloned.1.call-start = ((), (), s32[]{:S(2)}) async-start(), calls=%async_computation.4 | async-start | bytes 1310720 | tf_op jit(solution)/shard_map/all_gather | solution.py:24
  7.2 3.6 copy-start.7
  10.8 13.0 %copy-start.14 = (s32[1,16]{1,0:T(1,128)S(1)}, s32[1,16]{1,0:T(1,128)}, u32[]{:S(2)}) copy-start(s32[1,16]{1,0:T(1,128)} %param.33) | copy-start | bytes 196
  10.8 13.0 %copy-start.16 = (s32[1,16]{1,0:T(1,128)S(1)}, s32[1,16]{1,0:T(1,128)}, u32[]{:S(2)}) copy-start(s32[1,16]{1,0:T(1,128)} %param.32) | copy-start | bytes 196
  10.8 13.2 %copy-start.11 = (bf16[4,1024]{1,0:T(4,128)(2,1)S(1)}, bf16[4,1024]{1,0:T(4,128)(2,1)}, u32[]{:S(2)}) copy-start(bf16[4,1024]{1,0:T(4,128)(2,1)} %param.21) | copy-start | bytes 24580
  10.8 13.2 %copy-start.17 = (bf16[2048,16]{0,1:T(8,128)(2,1)S(1)}, bf16[2048,16]{0,1:T(8,128)(2,1)}, u32[]{:S(2)}) copy-start(bf16[2048,16]{0,1:T(8,128)(2,1)} %param.22) | copy-start | bytes 196612
  10.8 13.2 %copy-start.18 = (bf16[16,256]{1,0:T(8,128)(2,1)S(1)}, bf16[16,256]{1,0:T(8,128)(2,1)}, u32[]{:S(2)}) copy-start(bf16[16,256]{1,0:T(8,128)(2,1)} %param.23) | copy-start | bytes 24580
  10.8 13.2 %copy-start.19 = (f32[256]{0:T(256)S(1)}, f32[256]{0:T(256)}, u32[]{:S(2)}) copy-start(f32[256]{0:T(256)} %param.24) | copy-start | bytes 3076
  18.1 1.3 copy-start.10
  19.4 17.3 %collective-permute-start = (bf16[3,1024]{1,0:T(4,128)(2,1)S(1)}, bf16[3,1024]{1,0:T(4,128)(2,1)S(1)}, u32[]{:S(2)}, u32[]{:S(2)}) collective-permute-start(bf16[3,1024]{1,0:T(4,128)(2,1)S(1)} %slice_bitcast_fusion.5), channel_id=1, source_target_pairs={{0,2},{2,4},{4,6},{1,3},{3,5},{5,7},{8,10},{10,12},{12,14},{9,11},... | collective-permute-start | bytes 18440 | tf_op jit(solution)/shard_map/ppermute | solution.py:18
  31.0 13.5 %copy-start.5 = (f32[16,1,64,256]{3,0,1,2:T(8,128)}, f32[16,1,64,256]{3,0,1,2:T(8,128)S(1)}, u32[]{:S(2)}) copy-start(f32[16,1,64,256]{3,0,1,2:T(8,128)S(1)} %fusion.49) | copy-start | bytes 3145732
  44.6 7.4 %copy-start.4 = (f32[16,64,1,1024]{3,1,0,2:T(8,128)}, f32[16,64,1,1024]{3,1,0,2:T(8,128)S(1)}, u32[]{:S(2)}) copy-start(f32[16,64,1,1024]{3,1,0,2:T(8,128)S(1)} %fusion.15) | copy-start | bytes 12582916
  52.0 21.1 %copy-start.15 = (bf16[512]{0:T(512)(128)(2,1)S(1)}, bf16[512]{0:T(512)(128)(2,1)}, u32[]{:S(2)}) copy-start(bf16[512]{0:T(512)(128)(2,1)} %param.26) | copy-start | bytes 3076
  65.6 3.2 copy-start.2
  70.1 87.9 %all-gather.9.cloned.1.call-start = ((), (), s32[]{:S(2)}) async-start(), calls=%async_computation.3 | async-start | bytes 6127616 | tf_op jit(solution)/shard_map/all_gather | solution.py:153
  70.9 147.7 %all-gather.7.cloned.1.call-start = ((), (), s32[]{:S(2)}) async-start(), calls=%async_computation.2 | async-start | bytes 6127616 | tf_op jit(solution)/shard_map/all_gather | solution.py:154
  71.6 212.9 %all-gather.5.cloned.1.call-start = ((), (), s32[]{:S(2)}) async-start(), calls=%async_computation.1 | async-start | bytes 6127616 | tf_op jit(solution)/shard_map/all_gather | solution.py:155
  72.2 252.8 %all-reduce.3.cloned.1.call-start = ((), (), s32[]{:S(2)}) async-start(), calls=%async_computation.5 | async-start | bytes 8388608 | tf_op jit(solution)/shard_map/psum | solution.py:205
  158.0 8.2 %copy-start.3 = (f32[16,256,512]{2,0,1:T(8,128)S(1)}, f32[16,256,512]{2,0,1:T(8,128)}, u32[]{:S(2)}) copy-start(f32[16,256,512]{2,0,1:T(8,128)} %multiply_bitcast_fusion) | copy-start | bytes 25165828
  158.0 8.2 %copy-start.6 = (f32[16,1,64,256]{3,0,1,2:T(8,128)S(1)}, f32[16,1,64,256]{3,0,1,2:T(8,128)}, u32[]{:S(2)}) copy-start(f32[16,1,64,256]{3,0,1,2:T(8,128)} %copy-done.5) | copy-start | bytes 3145732
  158.0 8.2 %copy-start.8 = (f32[16,1,64,256]{3,2,0,1:T(8,128)S(1)}, f32[16,1,64,256]{3,2,0,1:T(8,128)}, u32[]{:S(2)}) copy-start(f32[16,1,64,256]{3,2,0,1:T(8,128)} %multiply_bitcast_fusion.1) | copy-start | bytes 3145732
  290.1 0.7 copy-start.13
  290.2 90.2 %reduce-scatter.2.cloned.1.call-start = ((), (), s32[]{:S(2)}) async-start(), calls=%async_computation.6 | async-start | bytes 6291456 | tf_op jit(solution)/shard_map/reduce_scatter | solution.py:217
  330.5 2.0 copy-start.9
  370.0 14.8 %copy-start.1 = (bf16[512,2048]{1,0:T(8,128)(2,1)S(1)}, bf16[512,2048]{1,0:T(8,128)(2,1)}, u32[]{:S(2)}) copy-start(bf16[512,2048]{1,0:T(8,128)(2,1)} %param.27) | copy-start | bytes 6291460
Sparse Core Ops, SparseCore 0:
  70.2 25.4 all-gather.10
  97.9 60.0 all-gather.8
  160.1 58.4 all-gather.6
  220.6 63.9 all-gather.4
  290.3 34.7 all-reduce.2
  364.2 16.0 reduce-scatter.1
where the time goes:
time: 398 us; the launch traced here: 392 us
  waiting for transfers between devices  203 us (51%)
  matrix products  100 us (25%)
  other arithmetic  45.1 us (11%)
  local copies, waits for them, and re-layouts  17 us (4%)
  between operations  15 us (4%)
  blocking collectives  6.9 us (2%)
  starting transfers between devices  4.61 us (1%)
    all_gather x1, waiting for transfers between devices, on_device(): gate_rows = lax.all_gather(gate_weight, 'req', axis=0, tiled=True)  62 us
    all_gather x1, waiting for transfers between devices, on_device(): down_columns = lax.all_gather(down_weight, 'req', axis=1, tiled=True)  56.9 us
    all_gather x1, waiting for transfers between devices, on_device(): up_rows = lax.all_gather(up_weight, 'req', axis=0, tiled=True)  38 us
    psum x1, waiting for transfers between devices, on_device(): lax.psum(partial_value.astype(jnp.bfloat16), 'hid').astype(jnp.float32)  34.2 us
    dot_general x1, matrix products, on_device(): partials = jnp.dot(hidden, down_columns, preferred_element_type=jnp.float32)  20.9 us
    dot_general x1, matrix products, page_block(): jnp.einsum('pqhe,qheb->pheb', weights, page_terms, precision=TOP_PRECISION)  13.6 us
    unnamed x43, local copies, waits for them, and re-layouts  12.8 us
    dot_general x1, matrix products, widen(): return jnp.dot(feed_in, weight_rows, preferred_element_type=jnp.float32)  10.7 us
  transfers between devices with their start and end apart: 7, of which 6 were waited for; matrix products, arithmetic and copies ran while one was open for 17% of the time, Pallas kernels for 0%

commit v1 on v0

--- a/solution.py
+++ b/solution.py
@@ -151,7 +151,9 @@
     )
     query_rows, key_rows, value_matrix = split_features(mixed_rows, HK)
     gate_rows = lax.all_gather(gate_weight, "req", axis=0, tiled=True)
-    up_rows = lax.all_gather(up_weight, "req", axis=0, tiled=True)
+    up_rows = jnp.concatenate(
+        lax.all_to_all(jnp.stack([up_weight] * lax.axis_size("req")), "req", 0, 0), axis=0
+    )
     down_columns = lax.all_gather(down_weight, "req", axis=1, tiled=True)
     gate_rows, query_rows = lax.optimization_barrier((gate_rows, query_rows))
     lowrank = jnp.dot(normed, decay_down, preferred_element_type=jnp.float32).astype(jnp.bfloat16)

time: 398 us -> 381 us (0.957)
  waiting for transfers between devices: 203 us -> 175 us
  starting transfers between devices: 4.61 us -> 11.5 us
    all_gather x1 -> x0, waiting for transfers between devices: 38 us -> none  [on_device(): up_rows = lax.all_gather(up_weight, 'req', axis=0, tiled=True)]
    all_gather x1, waiting for transfers between devices: 62 us -> 99.3 us  [on_device(): gate_rows = lax.all_gather(gate_weight, 'req', axis=0, tiled=True)]
    all_gather x1, waiting for transfers between devices: 56.9 us -> 34.3 us  [on_device(): down_columns = lax.all_gather(down_weight, 'req', axis=1, tiled=True)]
    all_to_all x0 -> x1, starting transfers between devices: none -> 6.93 us  [on_device(): lax.all_to_all(jnp.stack([up_weight] * lax.axis_size('req')), 'req', 0, 0)]
    all_gather x1, waiting for transfers between devices: 4.1 us -> 0.01 us  [prefix_2(): lax.all_gather(a.astype(kind), axis)]
    unnamed x43 -> x45, local copies, waits for them, and re-layouts: 12.8 us -> 12.8 us
  transfers between devices with their start and end apart: 7 -> 7, of which waited for: 6 -> 4; matrix products, arithmetic and copies ran while one was open for 17% -> 19% of each run, Pallas kernels for 0% -> 0%
where the time goes in v1:
time: 381 us; the launch traced here: 375 us
  waiting for transfers between devices  175 us (46%)
  matrix products  101 us (27%)
  other arithmetic  44.9 us (12%)
  local copies, waits for them, and re-layouts  20.1 us (5%)
  between operations  14.7 us (4%)
  starting transfers between devices  11.5 us (3%)
  blocking collectives  7.68 us (2%)
    all_gather x1, waiting for transfers between devices, on_device(): gate_rows = lax.all_gather(gate_weight, 'req', axis=0, tiled=True)  99.3 us
    all_gather x1, waiting for transfers between devices, on_device(): down_columns = lax.all_gather(down_weight, 'req', axis=1, tiled=True)  34.3 us
    psum x1, waiting for transfers between devices, on_device(): lax.psum(partial_value.astype(jnp.bfloat16), 'hid').astype(jnp.float32)  34.2 us
    dot_general x1, matrix products, on_device(): partials = jnp.dot(hidden, down_columns, preferred_element_type=jnp.float32)  20.9 us
    dot_general x1, matrix products, page_block(): jnp.einsum('pqhe,qheb->pheb', weights, page_terms, precision=TOP_PRECISION)  13.6 us
    unnamed x45, local copies, waits for them, and re-layouts  12.8 us
    dot_general x1, matrix products, widen(): return jnp.dot(feed_in, weight_rows, preferred_element_type=jnp.float32)  10.8 us
    dot_general x1, matrix products, page_block(): jnp.einsum('phik,phkv->phiv', raised_rows, previous, precision=TOP_PRECIS...  10.6 us
  transfers between devices with their start and end apart: 7, of which 4 were waited for; matrix products, arithmetic and copies ran while one was open for 19% of the time, Pallas kernels for 0%

profile of v1, /device:TPU:1, one launch (start us, length us, event | category | flops | bytes accessed | tf_op | source)
XLA Modules:
  0.0 374.7 jit_solution(18434760056850101774)
XLA Ops:
  7.2 3.2 fusion.3
  10.5 0.3 copy-done.7
  10.8 7.3 %convolution_convert_fusion.2 = bf16[1024,1024]{1,0:T(8,128)(2,1)S(1)} fusion(bf16[2048,1024]{1,0:T(8,128)(2,1)} %param.20, bf16[1024,2048]{1,0:T(8,128)(2,1)S(1)} %copy-done.7, f32[2048]{0:T(1024)S(1)} %convert_element_type.149, f32[1024]{0:T(1024)S(1)} %add_rsqrt_fusion.2), kind=kOutput, calls=%fused_computation.53 | convolution fusion | flops 4304404480 | bytes 10498048 | tf_op jit(solution)/shard_map/dot_general | solution.py:143
  18.1 1.3 copy-done.10
  19.4 4.4 %collective-permute-start = (bf16[3,1024]{1,0:T(4,128)(2,1)S(1)}, bf16[3,1024]{1,0:T(4,128)(2,1)S(1)}, u32[]{:S(2)}, u32[]{:S(2)}) collective-permute-start(bf16[3,1024]{1,0:T(4,128)(2,1)S(1)} %slice_bitcast_fusion.5), channel_id=1, source_target_pairs={{0,2},{2,4},{4,6},{1,3},{3,5},{5,7},{8,10},{10,12},{12,14},{9,11},... | collective-permute-start | bytes 18440 | tf_op jit(solution)/shard_map/ppermute | solution.py:18
  24.0 5.2 %fusion.37 = f32[1024,256]{1,0:T(8,128)} fusion(bf16[16,256]{1,0:T(8,128)(2,1)S(1)} %copy-done.19, bf16[2048,16]{0,1:T(8,128)(2,1)S(1)} %copy-done.18, f32[256]{0:T(256)S(1)} %copy-done.20, bf16[1024,2048]{1,0:T(8,128)(2,1)} %param.18, f32[2048]{0:T(1024)S(1)} %convert_element_type.149, f32[1024]{0:T(1024)S(1)} %add_rsqrt_fusion.2), kind=kOutput, calls=%fused_computation.60 | convolution fusion | flops 86523904 | bytes 5329920 | tf_op jit(solution)/shard_map/dot_general | solution.py:162
  29.2 1.8 fusion.49
  31.4 0.1 reduce.2
  31.6 1.0 slice.80
  32.6 4.1 %convert_element_type.152 = f32[16,64,1024]{2,1,0:T(8,128)} convert(bf16[16,64,1024]{2,1,0:T(8,128)(2,1)} %bitcast.124) | non-fusion elementwise | flops 1048576 | bytes 6291456 | tf_op jit(solution)/shard_map/convert_element_type | solution.py:63
  36.9 7.5 %fusion.15 = f32[16,64,1,1024]{3,1,0,2:T(8,128)S(1)} fusion(f32[16,64,1024]{2,1,0:T(8,128)} %convert_element_type.152, f32[16,3,1024]{2,1,0:T(4,128)S(1)} %convert_multiply_fusion.4, f32[1024]{0:T(1024)S(1)} %bitcast.131, f32[1024]{0:T(1024)S(1)} %bitcast.132, f32[1024]{0:T(1024)S(1)} %bitcast.130, f32[1024]{0:T(1024)S(1)} %bitcast.129), kind=kLoop, calls=%fused_computation.29 | loop fusion | flops 10485760 | bytes 8601600 | tf_op jit(solution)/shard_map/reshape | solution.py:149
  44.5 7.4 %fusion.30 = f32[16,256,512]{2,1,0:T(8,128)S(1)} fusion(f32[16,64,1,1024]{3,1,0,2:T(8,128)S(1)} %fusion.15, f32[16,1,64,256]{3,0,1,2:T(8,128)S(1)} %fusion.49, f32[16,256]{1,0:T(8,128)S(1)} %get-tuple-element.97), kind=kOutput, calls=%fused_computation.51 | convolution fusion | flops 1612447744 | bytes 12599296 | tf_op jit(solution)/shard_map/phte,phtb->pheb/dot_general | solution.py:99
  51.9 13.6 %fusion.20 = f32[16,1,256,512]{3,0,2,1:T(8,128)S(1)} fusion(f32[16,256,512]{2,1,0:T(8,128)S(1)} %fusion.30, f32[16,256]{0,1:T(8,128)S(1)} %bitcast.126, pred[16,16]{1,0:T(8,128)(4,1)S(1)} %fusion.72), kind=kOutput, calls=%fused_computation.38 | convolution fusion | flops 402849792 | bytes 16793856 | tf_op jit(solution)/shard_map/pqhe,qheb->pheb/dot_general | solution.py:107
  65.5 3.2 copy-done.2
  68.8 0.6 slice.145
  69.3 0.8 copy.72
  70.1 0.7 all-gather.6.cloned.1.call-update
  70.9 0.7 all-gather.4.cloned.1.call-update
  71.6 3.0 stack.2
  74.6 6.9 %all-to-all-start = ((bf16[16,128,1408]{2,1,0:T(8,128)(2,1)}), bf16[16,128,1408]{2,1,0:T(8,128)(2,1)}, u32[]{:S(2)}, u32[]{:S(2)}) async-start(bf16[16,128,1408]{2,1,0:T(8,128)(2,1)} %stack.2), calls=%async_computation | async-start | bytes 11534336 | tf_op jit(solution)/shard_map/all_to_all | solution.py:155
  81.8 0.5 slice.90
  82.3 0.1 reduce.3
  82.4 0.6 fusion.74
  83.0 7.7 %all_gather.16 = bf16[4,1,256]{2,1,0:T(2,128)(2,1)S(1)} all-gather(bf16[1,1,256]{2,1,0:T(2,128)(2,1)S(1)} %fusion.74), channel_id=1, replica_groups=mesh['req'=16,'seq'=4,'hid'=2] {'seq'}, dimensions={0}, use_global_device_ids=true | all-gather | bytes 2560 | tf_op jit(solution)/shard_map/all_gather | solution.py:24
  90.7 2.5 multiply_bitcast_fusion.1
  93.2 8.5 %multiply_bitcast_fusion = f32[16,256,512]{2,0,1:T(8,128)} fusion(f32[15,1,256,512]{3,0,2,1:T(8,128)} %bitcast.120, f32[16]{0:T(128)S(1)} %get-tuple-element.95), kind=kLoop, calls=%fused_computation.19 | loop fusion | flops 2097152 | bytes 16252992 | tf_op jit(solution)/shard_map/reshape.35
  101.8 0.2 while.12
  102.0 99.3 %all-gather.6.cloned.1.call-done = bf16[2048,1408]{1,0:T(8,128)(2,1)} async-done(((bf16[128,1408]{1,0:T(8,128)(2,1)}), bf16[2048,1408]{1,0:T(8,128)(2,1)}) %all-gather.6.cloned.1.call-update) | async-done | bytes 5767184 | tf_op jit(solution)/shard_map/all_gather | solution.py:153
  201.3 4.7 %convolution_select_fusion = f32[16,64,64]{2,1,0:T(8,128)S(1)} fusion(f32[16,1,64,256]{3,2,0,1:T(8,128)} %multiply_bitcast_fusion.1, f32[16,1,64,256]{3,0,1,2:T(8,128)} %copy-done.5, pred[64,64]{1,0:T(8,128)(4,1)S(1)} %iota_compare_fusion, f32[16,64,1,1024]{3,1,0,2:T(8,128)} %copy-done.4), kind=kOutput, calls=%fused_computation.56 | convolution fusion | flops 203489280 | bytes 4460544 | tf_op jit(solution)/shard_map/phik,phjk->phij/dot_general | solution.py:92
  206.1 3.4 fusion.31
  209.5 10.6 %fusion.7 = f32[16,64,512]{2,1,0:T(8,128)S(1)} fusion(f32[16,256,512]{2,0,1:T(8,128)S(1)} %copy-done.3, f32[16,1,64,256]{3,2,0,1:T(8,128)S(1)} %copy-done.8, f32[16,1,64,256]{3,0,1,2:T(8,128)S(1)} %copy-done.6), kind=kOutput, calls=%fused_computation.14 | convolution fusion | flops 1610874880 | bytes 12582912 | tf_op jit(solution)/shard_map/phik,phkv->phiv/dot_general | solution.py:110
  220.1 3.9 %bitcast_add_fusion = f32[16,1,64,512]{3,2,0,1:T(8,128)} fusion(f32[16,64,512]{2,1,0:T(8,128)S(1)} %fusion.31, f32[16,64,512]{2,1,0:T(8,128)S(1)} %fusion.7, f32[16,1,64,256]{3,2,0,1:T(8,128)S(1)} %copy-done.8, f32[16,1,64,256]{3,0,1,2:T(8,128)S(1)} %copy-done.6, f32[1,256,512]{2,1,0:T(8,128)S(1)} %get-tuple-element.54, ...), kind=kOutput, calls=%fused_computation.41 | convolution fusion | flops 1612447744 | bytes 8929344 | tf_op jit(solution)/shard_map/dlof,lfg->dlog/dot_general | solution.py:188
  224.0 1.8 multiply_reduce_fusion
  225.9 7.2 %fusion.25 = bf16[1024,512]{1,0:T(8,128)(2,1)} fusion(f32[16,1,64,512]{3,2,0,1:T(8,128)} %bitcast_add_fusion, f32[512]{0:T(512)S(1)} %convert_element_type.163, f32[1024]{0:T(1024)S(1)} %rsqrt.29, bf16[2048,512]{1,0:T(8,128)(2,1)} %param.25, bf16[1024,2048]{1,0:T(8,128)(2,1)} %param.18, f32[2048]{0:T(1024)S(1)} %convert_element_type.149, ...), kind=kOutput, calls=%fused_computation.45 | convolution fusion | flops 2160066560 | bytes 9455616 | tf_op jit(solution)/shard_map/dot_general | solution.py:197
  233.1 34.3 %all-gather.4.cloned.1.call-done = bf16[1408,2048]{1,0:T(8,128)(2,1)} async-done(((bf16[1408,128]{1,0:T(8,128)(2,1)}), bf16[1408,2048]{1,0:T(8,128)(2,1)}) %all-gather.4.cloned.1.call-update) | async-done | bytes 5767184 | tf_op jit(solution)/shard_map/all_gather | solution.py:157
  267.4 5.6 %convolution_convert_fusion.1 = bf16[1024,2048]{1,0:T(8,128)(2,1)} fusion(bf16[1024,512]{1,0:T(8,128)(2,1)} %fusion.25, bf16[512,2048]{1,0:T(8,128)(2,1)S(1)} %copy-done), kind=kOutput, calls=%fused_computation.37 | convolution fusion | flops 2149580800 | bytes 7340032 | tf_op jit(solution)/shard_map/dot_general | solution.py:204
  273.1 0.6 copy-done.14
  273.7 34.2 %all-reduce.3.cloned.1.call-done = bf16[1024,2048]{1,0:T(8,128)(2,1)} async-done(((bf16[1024,2048]{1,0:T(8,128)(2,1)}), bf16[1024,2048]{1,0:T(8,128)(2,1)}) %all-reduce.3.cloned.1.call-update) | async-done | bytes 4194320 | tf_op jit(solution)/shard_map/psum | solution.py:207
  307.9 5.5 %fusion = (f32[1024]{0:T(1024)S(1)}, bf16[1024,2048]{1,0:T(8,128)(2,1)S(1)}) fusion(bf16[1024,2048]{1,0:T(8,128)(2,1)} %all-reduce.3.cloned.1.call-done, bf16[1024,2048]{1,0:T(8,128)(2,1)} %param.18), kind=kLoop, calls=%fused_computation.7 | loop fusion | flops 14679040 | bytes 12587008 | tf_op jit(solution)/shard_map/reduce_sum | solution.py:45
  313.4 2.0 copy-done.9
  315.4 10.8 %fusion.34 = f32[1024,1408]{1,0:T(8,128)} fusion(bf16[2048,1408]{1,0:T(8,128)(2,1)} %all-gather.6.cloned.1.call-done, bf16[1024,2048]{1,0:T(8,128)(2,1)S(1)} %get-tuple-element.93, f32[2048]{0:T(1024)S(1)} %convert_element_type.170, f32[1024]{0:T(1024)S(1)} %add_rsqrt_fusion.1), kind=kOutput, calls=%fused_computation.57 | convolution fusion | flops 5913968640 | bytes 15740928 | tf_op jit(solution)/shard_map/dot_general | solution.py:213
  326.2 20.9 %convolution_convert_fusion = bf16[1024,2048]{1,0:T(8,128)(2,1)} fusion(bf16[1408,2048]{1,0:T(8,128)(2,1)} %all-gather.4.cloned.1.call-done, f32[1024,1408]{1,0:T(8,128)} %fusion.34, bf16[2048,1408]{1,0:T(8,128)(2,1)} %bitcast.2, bf16[1024,2048]{1,0:T(8,128)(2,1)} %copy-done.9, f32[2048]{0:T(1024)S(1)} %convert_element_type.170, f32[1024]{0:T(1024)S(1)} %add_rsqrt_fusion.1), kind=kOutput, calls=%fused_computation.36 | convolution fusion | flops 11830296576 | bytes 25702400 | tf_op jit(solution)/shard_map/dot_general | solution.py:218
  347.2 1.0 slice.93
  348.4 0.7 copy.76
  349.1 4.0 %add_convert_fusion = bf16[16,1,256,512]{3,0,2,1:T(8,128)(2,1)S(1)} fusion(f32[16,1,256,512]{3,0,2,1:T(8,128)} %copy-done.2, f32[256,512]{1,0:T(8,128)S(1)} %bitcast.121, f32[16,256]{0,1:T(8,128)S(1)} %copy.74), kind=kLoop, calls=%fused_computation.18 | loop fusion | flops 6291456 | bytes 13123584 | tf_op jit(solution)/shard_map/convert_element_type | solution.py:223
  353.1 4.5 %copy.75 = bf16[16,1,256,512]{3,2,1,0:T(8,128)(2,1)} copy(bf16[16,1,256,512]{3,0,2,1:T(8,128)(2,1)S(1)} %add_convert_fusion) | data formatting | bytes 8388608
  357.5 5.8 %reduce-scatter.2.cloned.1.call-done = bf16[512,2048]{1,0:T(8,128)(2,1)} async-done(((bf16[1024,2048]{1,0:T(8,128)(2,1)}), bf16[512,2048]{1,0:T(8,128)(2,1)}) %reduce-scatter.2.cloned.1.call-update) | async-done | bytes 2097168 | tf_op jit(solution)/shard_map/reduce_scatter | solution.py:219
  363.3 4.4 %add_convert_fusion.1 = bf16[512,2048]{1,0:T(8,128)(2,1)} fusion(bf16[512,2048]{1,0:T(8,128)(2,1)} %reduce-scatter.2.cloned.1.call-done, bf16[1024,2048]{1,0:T(8,128)(2,1)} %copy-done.9, s32[]{:T(128)S(6)} %select_n.46), kind=kLoop, calls=%fused_computation.35 | loop fusion | flops 4194304 | bytes 6291460 | tf_op jit(solution)/shard_map/convert_element_type | solution.py:222
  (76 shorter events, 1.5 us)
Async XLA Ops:
  7.2 260.2 %copy-start = (bf16[512,2048]{1,0:T(8,128)(2,1)S(1)}, bf16[512,2048]{1,0:T(8,128)(2,1)}, u32[]{:S(2)}) copy-start(bf16[512,2048]{1,0:T(8,128)(2,1)} %param.27) | copy-start | bytes 6291460
  7.2 3.3 copy-start.13
  7.2 94.6 %all-gather.8.cloned.1.call-start = ((), (), s32[]{:S(2)}) async-start(), calls=%async_computation.4 | async-start | bytes 1310720 | tf_op jit(solution)/shard_map/all_gather | solution.py:24
  7.2 3.6 copy-start.7
  10.8 13.0 %copy-start.15 = (s32[1,16]{1,0:T(1,128)S(1)}, s32[1,16]{1,0:T(1,128)}, u32[]{:S(2)}) copy-start(s32[1,16]{1,0:T(1,128)} %param.33) | copy-start | bytes 196
  10.8 13.0 %copy-start.17 = (s32[1,16]{1,0:T(1,128)S(1)}, s32[1,16]{1,0:T(1,128)}, u32[]{:S(2)}) copy-start(s32[1,16]{1,0:T(1,128)} %param.32) | copy-start | bytes 196
  10.8 13.2 %copy-start.12 = (bf16[4,1024]{1,0:T(4,128)(2,1)S(1)}, bf16[4,1024]{1,0:T(4,128)(2,1)}, u32[]{:S(2)}) copy-start(bf16[4,1024]{1,0:T(4,128)(2,1)} %param.21) | copy-start | bytes 24580
  10.8 13.2 %copy-start.18 = (bf16[2048,16]{0,1:T(8,128)(2,1)S(1)}, bf16[2048,16]{0,1:T(8,128)(2,1)}, u32[]{:S(2)}) copy-start(bf16[2048,16]{0,1:T(8,128)(2,1)} %param.22) | copy-start | bytes 196612
  10.8 13.2 %copy-start.19 = (bf16[16,256]{1,0:T(8,128)(2,1)S(1)}, bf16[16,256]{1,0:T(8,128)(2,1)}, u32[]{:S(2)}) copy-start(bf16[16,256]{1,0:T(8,128)(2,1)} %param.23) | copy-start | bytes 24580
  10.8 13.2 %copy-start.20 = (f32[256]{0:T(256)S(1)}, f32[256]{0:T(256)}, u32[]{:S(2)}) copy-start(f32[256]{0:T(256)} %param.24) | copy-start | bytes 3076
  18.1 1.3 copy-start.10
  19.4 17.3 %collective-permute-start = (bf16[3,1024]{1,0:T(4,128)(2,1)S(1)}, bf16[3,1024]{1,0:T(4,128)(2,1)S(1)}, u32[]{:S(2)}, u32[]{:S(2)}) collective-permute-start(bf16[3,1024]{1,0:T(4,128)(2,1)S(1)} %slice_bitcast_fusion.5), channel_id=1, source_target_pairs={{0,2},{2,4},{4,6},{1,3},{3,5},{5,7},{8,10},{10,12},{12,14},{9,11},... | collective-permute-start | bytes 18440 | tf_op jit(solution)/shard_map/ppermute | solution.py:18
  31.0 13.4 %copy-start.5 = (f32[16,1,64,256]{3,0,1,2:T(8,128)}, f32[16,1,64,256]{3,0,1,2:T(8,128)S(1)}, u32[]{:S(2)}) copy-start(f32[16,1,64,256]{3,0,1,2:T(8,128)S(1)} %fusion.49) | copy-start | bytes 3145732
  44.5 7.4 %copy-start.4 = (f32[16,64,1,1024]{3,1,0,2:T(8,128)}, f32[16,64,1,1024]{3,1,0,2:T(8,128)S(1)}, u32[]{:S(2)}) copy-start(f32[16,64,1,1024]{3,1,0,2:T(8,128)S(1)} %fusion.15) | copy-start | bytes 12582916
  51.9 19.7 %copy-start.11 = (bf16[128,1408]{1,0:T(8,128)(2,1)S(1)}, bf16[128,1408]{1,0:T(8,128)(2,1)}, u32[]{:S(2)}) copy-start(bf16[128,1408]{1,0:T(8,128)(2,1)} %param.30) | copy-start | bytes 1081348
  65.5 3.2 copy-start.2
  70.1 131.2 %all-gather.6.cloned.1.call-start = ((), (), s32[]{:S(2)}) async-start(), calls=%async_computation.3 | async-start | bytes 6127616 | tf_op jit(solution)/shard_map/all_gather | solution.py:153
  70.9 196.6 %all-gather.4.cloned.1.call-start = ((), (), s32[]{:S(2)}) async-start(), calls=%async_computation.2 | async-start | bytes 6127616 | tf_op jit(solution)/shard_map/all_gather | solution.py:157
  74.6 7.8 %copy-start.16 = (bf16[512]{0:T(512)(128)(2,1)S(1)}, bf16[512]{0:T(512)(128)(2,1)}, u32[]{:S(2)}) copy-start(bf16[512]{0:T(512)(128)(2,1)} %param.26) | copy-start | bytes 3076
  74.6 149.3 %all-to-all-start = ((bf16[16,128,1408]{2,1,0:T(8,128)(2,1)}), bf16[16,128,1408]{2,1,0:T(8,128)(2,1)}, u32[]{:S(2)}, u32[]{:S(2)}) async-start(bf16[16,128,1408]{2,1,0:T(8,128)(2,1)} %stack.2), calls=%async_computation | async-start | bytes 11534336 | tf_op jit(solution)/shard_map/all_to_all | solution.py:155
  81.6 226.3 %all-reduce.3.cloned.1.call-start = ((), (), s32[]{:S(2)}) async-start(), calls=%async_computation.5 | async-start | bytes 8388608 | tf_op jit(solution)/shard_map/psum | solution.py:207
  201.3 8.2 %copy-start.3 = (f32[16,256,512]{2,0,1:T(8,128)S(1)}, f32[16,256,512]{2,0,1:T(8,128)}, u32[]{:S(2)}) copy-start(f32[16,256,512]{2,0,1:T(8,128)} %multiply_bitcast_fusion) | copy-start | bytes 25165828
  201.3 8.2 %copy-start.6 = (f32[16,1,64,256]{3,0,1,2:T(8,128)S(1)}, f32[16,1,64,256]{3,0,1,2:T(8,128)}, u32[]{:S(2)}) copy-start(f32[16,1,64,256]{3,0,1,2:T(8,128)} %copy-done.5) | copy-start | bytes 3145732
  201.3 8.2 %copy-start.8 = (f32[16,1,64,256]{3,2,0,1:T(8,128)S(1)}, f32[16,1,64,256]{3,2,0,1:T(8,128)}, u32[]{:S(2)}) copy-start(f32[16,1,64,256]{3,2,0,1:T(8,128)} %multiply_bitcast_fusion.1) | copy-start | bytes 3145732
  273.0 0.7 copy-start.14
  273.0 90.3 %reduce-scatter.2.cloned.1.call-start = ((), (), s32[]{:S(2)}) async-start(), calls=%async_computation.6 | async-start | bytes 6291456 | tf_op jit(solution)/shard_map/reduce_scatter | solution.py:219
  313.4 2.1 copy-start.9
  353.0 14.7 %copy-start.1 = (bf16[512,2048]{1,0:T(8,128)(2,1)S(1)}, bf16[512,2048]{1,0:T(8,128)(2,1)}, u32[]{:S(2)}) copy-start(bf16[512,2048]{1,0:T(8,128)(2,1)} %param.27) | copy-start | bytes 6291460
Sparse Core Ops, SparseCore 0:
  70.2 25.4 all-gather.7
  97.9 103.3 all-gather.5
  203.4 63.9 all-gather.3
  273.1 34.7 all-reduce.2
  347.3 15.9 reduce-scatter.1
